TPU v7x, 128 devices: a whole 4x4x4 slice. The times are simulated.
128 devices in a mesh: row: 8 (over x, core), col: 16 (over z, y).
Axes of the slice: x: 4, y: 4, z: 4, core: 2. Of those that a mesh axis runs over, the one named last changes fastest.
Arguments:
- density_tiles: float32 [3, 4096, 4096], P(None, ('row', 'col')), may hold values from -0.012 to 0.012
- tile_ids: int32 [4096], P(('row', 'col')), may hold values from 0 to 16383, as said below
- batch_blocks: int32 [128, 8], replicated, may hold values from 0 to 127, as said below
- basis_values: float32 [128, 512, 1024], P(('row', 'col')), may hold values from -6 to 6
- grid_weight: float32 [128, 1024], P(('row', 'col')), may hold values from 0.0002 to 0.002
- xc_kernel: float32 [128, 1024], P(('row', 'col')), may hold values from -2 to -0.5
- grid_coord: float32 [3, 128, 1024], P(None, ('row', 'col')), may hold values from -1 to 1
- orbitals: float32 [8192, 512], P('row'), may hold values from -1.5 to 1.5
- precond_diag: float32 [8192], P('row'), may hold values from 1 to 4
- orbital_energy: float32 [512], replicated, may hold values from -3 to -0.5
Outputs:
- new_density: float32 [3, 4096, 4096], P(None, ('row', 'col'))
Inputs may be any that keep to these rules, and one draw needn't show every extreme that they name: `tile_ids`: the 32 slots of device (r, c), counted in row+col order, list distinct tiles I * 128 + J with I in the r-th range of 16 blocks and J in the c-th range of 8 blocks. `batch_blocks`: each row holds 8 ascending blocks, no two in the same range of 8 blocks, and exactly 1 of them in each range of 16 blocks.
All inputs are finite; a program needn't handle non-finite values.
Results may differ from a plain program's by a relative error of at most 0.0003.
Values sent between devices are 32-bit elements; how exact they have to be, the bound alone decides.
A program may use at most 128 MiB of HBM per device.

v0:
```python
import jax
import jax.numpy as jnp
from jax import lax
from jax.sharding import PartitionSpec as P

NB = 8192
TILE = 64
FB = 8
PRECISE = lax.Precision.HIGHEST


def from_root(value, axis, source):
    kept = jnp.where(lax.axis_index(axis) == source, value, 0).astype(value.dtype)
    return lax.psum(kept, axis)


def slot_plan(blocks, owner_row, owner_col, col_blocks, per_range):
    matched = blocks // col_blocks == owner_col[..., None]
    active = jnp.any(matched, axis=-1)
    positions = jnp.arange(blocks.shape[-1], dtype=jnp.int32)
    column_place = jnp.sum(jnp.where(matched, positions, 0), axis=-1)
    row_place = owner_row[..., None] * per_range + jnp.arange(per_range, dtype=jnp.int32)
    return (active, row_place, column_place)


def local(
    density_tiles,
    tile_ids,
    batch_blocks,
    basis_values,
    grid_weight,
    xc_kernel,
    grid_coord,
    orbitals,
    precond_diag,
    orbital_energy,
):
    row_count = lax.axis_size("row")
    col_count = lax.axis_size("col")
    device_count = row_count * col_count
    own_row = lax.axis_index("row")
    own_col = lax.axis_index("col")
    own_index = own_row * col_count + own_col
    block_count = NB // TILE
    row_blocks = block_count // row_count
    col_blocks = block_count // col_count
    per_range = FB // row_count
    batch_count = basis_values.shape[0]
    slot_count = batch_count * per_range
    tile_area = TILE * TILE
    tile_local = tile_ids.shape[0]
    orbital_count = orbitals.shape[1]
    col_ratio = col_count // row_count
    col_width = col_blocks * TILE
    batch_width = FB * TILE
    orbital_piece = lax.dynamic_slice_in_dim(
        orbitals, own_col % col_ratio * col_width, col_width, 0
    )
    orbital_cols = from_root(orbital_piece, "row", own_col // col_ratio)
    requests = batch_blocks.reshape(device_count, batch_count, FB)
    owner_rows = jnp.full((device_count, batch_count), own_row, dtype=jnp.int32)
    owner_cols = jnp.full((device_count, batch_count), own_col, dtype=jnp.int32)
    active, row_place, column_place = slot_plan(
        requests, owner_rows, owner_cols, col_blocks, per_range
    )
    want_rows = jnp.take_along_axis(requests, row_place, axis=2)
    want_col = jnp.take_along_axis(requests, column_place[..., None], axis=2)
    wanted = jnp.where(active[..., None], want_rows * block_count + want_col, -1).reshape(-1)
    selector = (wanted[:, None] == tile_ids[None, :]).astype(jnp.float32)
    outgoing = jnp.einsum("ns,dsx->dnx", selector, density_tiles, precision=PRECISE)
    arrived = lax.all_to_all(outgoing, ("row", "col"), split_axis=1, concat_axis=1, tiled=True)
    own_blocks = lax.dynamic_slice_in_dim(requests, own_index, 1, 0)[0]
    block_pos = jnp.arange(FB, dtype=jnp.int32)
    batch_pos = jnp.arange(batch_count, dtype=jnp.int32)
    source = (block_pos // per_range)[None, :, None] * col_count + (own_blocks // col_blocks)[
        :, None, :
    ]
    lookup = (
        source * slot_count
        + batch_pos[:, None, None] * per_range
        + (block_pos % per_range)[None, :, None]
    )
    density = jnp.take(arrived, lookup.reshape(-1), axis=1).reshape(
        3, batch_count, FB, FB, TILE, TILE
    )
    density = density.transpose(0, 1, 2, 4, 3, 5).reshape(3, batch_count, batch_width, batch_width)
    projected = jnp.einsum("dkmn,knp->dkmp", density, basis_values, precision=PRECISE)
    response = jnp.sum(basis_values[None] * projected, axis=2)
    potential = xc_kernel[None] * response + grid_coord
    weighted = basis_values[None] * (grid_weight[None] * potential)[:, :, None, :]
    hamiltonian = jnp.einsum("dkmp,knp->dkmn", weighted, basis_values, precision=PRECISE)
    ham_tiles = (
        hamiltonian.reshape(3, batch_count, FB, TILE, FB, TILE)
        .transpose(0, 1, 2, 4, 3, 5)
        .reshape(3, batch_count * FB * FB, tile_area)
    )
    owners = jnp.arange(device_count, dtype=jnp.int32)
    target_rows = (owners // col_count)[:, None]
    target_cols = (owners % col_count)[:, None]
    mine_all = jnp.broadcast_to(own_blocks[None], (device_count, batch_count, FB))
    back_active, back_rows, back_col = slot_plan(
        mine_all, target_rows, target_cols, col_blocks, per_range
    )
    pick_index = (batch_pos[None, :, None] * FB + back_rows) * FB + back_col[..., None]
    keep_mask = back_active[..., None].reshape(-1)
    returning = jnp.where(
        keep_mask[None, :, None], jnp.take(ham_tiles, pick_index.reshape(-1), axis=1), 0.0
    )
    returned = lax.all_to_all(returning, ("row", "col"), split_axis=1, concat_axis=1, tiled=True)
    ham_listed = jnp.einsum("ns,dnx->dsx", selector, returned, precision=PRECISE)
    local_rows = tile_ids // block_count - own_row * row_blocks
    local_cols = tile_ids % block_count - own_col * col_blocks
    row_hot = (local_rows[None, :] == jnp.arange(row_blocks, dtype=jnp.int32)[:, None]).astype(
        jnp.float32
    )
    col_hot = (local_cols[None, :] == jnp.arange(col_blocks, dtype=jnp.int32)[:, None]).astype(
        jnp.float32
    )
    block_matrix = jnp.einsum(
        "rs,cs,dsab->dracb",
        row_hot,
        col_hot,
        ham_listed.reshape(3, tile_local, TILE, TILE),
        precision=PRECISE,
    )
    block_matrix = block_matrix.reshape(3, row_blocks * TILE, col_width)
    partial_rows = jnp.einsum("drc,co->dro", block_matrix, orbital_cols, precision=PRECISE)
    summed_rows = lax.psum(partial_rows, "col")
    response_orbs = -summed_rows / (precond_diag[:, None] - orbital_energy[None, :])
    response_piece = lax.dynamic_slice_in_dim(
        response_orbs, own_col % col_ratio * col_width, col_width, 1
    )
    response_cols = from_root(response_piece, "row", own_col // col_ratio)
    x_rows = jnp.take(response_orbs.reshape(3, row_blocks, TILE, orbital_count), local_rows, axis=1)
    c_rows = jnp.take(orbitals.reshape(row_blocks, TILE, orbital_count), local_rows, axis=0)
    x_cols = jnp.take(response_cols.reshape(3, col_blocks, TILE, orbital_count), local_cols, axis=1)
    c_cols = jnp.take(orbital_cols.reshape(col_blocks, TILE, orbital_count), local_cols, axis=0)
    renewed = jnp.einsum("dsao,sbo->dsab", x_rows, c_cols, precision=PRECISE)
    renewed = renewed + jnp.einsum("sao,dsbo->dsab", c_rows, x_cols, precision=PRECISE)
    return renewed.reshape(3, tile_local, tile_area)


def solution(mesh):
    placed = (
        P(None, ("row", "col"), None),
        P(("row", "col")),
        P(),
        P(("row", "col"), None, None),
        P(("row", "col"), None),
        P(("row", "col"), None),
        P(None, ("row", "col"), None),
        P("row", None),
        P("row"),
        P(),
    )
    return jax.shard_map(
        local, mesh=mesh, in_specs=placed, out_specs=P(None, ("row", "col"), None), check_vma=False
    )
```

profile of v0, /device:TPU:0, one launch (start us, length us, event | category | flops | bytes accessed | tf_op | source)
XLA Modules:
  0.0 686.3 jit_solution(637120942322534087)
XLA Ops:
  6.5 1.0 dynamic-slice_reduce_fusion
  7.6 0.7 fusion.82
  8.6 1.8 gather_fusion.7
  10.4 1.8 gather_fusion.6
  12.1 3.4 convolution_bitcast_fusion
  15.5 7.5 %copy.47 = f32[3,128,4096]{2,0,1:T(4,128)} copy(f32[3,128,4096]{2,1,0:T(8,128)S(1)} %convolution_bitcast_fusion) | data formatting | bytes 12582912 | tf_op jit(solution)/shard_map/ns,dsx->dnx/transpose | solution.py:70
  23.1 12.2 %all-to-all-start = ((f32[3,128,4096]{2,0,1:T(4,128)}), f32[3,128,4096]{2,0,1:T(4,128)}, u32[]{:S(2)}, u32[]{:S(2)}) async-start(f32[3,128,4096]{2,0,1:T(4,128)} %copy.47), calls=%async_computation | async-start | bytes 16777216 | tf_op jit(solution)/shard_map/all_to_all | solution.py:71
  35.5 0.1 fusion.61
  35.7 103.5 %all-to-all-done = f32[3,128,4096]{2,0,1:T(4,128)} async-done(((f32[3,128,4096]{2,0,1:T(4,128)}), f32[3,128,4096]{2,0,1:T(4,128)}, u32[]{:S(2)}, u32[]{:S(2)}) %all-to-all-start) | async-done | bytes 6291488 | tf_op jit(solution)/shard_map/all_to_all | solution.py:71
  139.2 8.1 %gather_fusion.1 = f32[64,3,4096]{2,1,0:T(4,128)} fusion(f32[3,128,4096]{2,0,1:T(4,128)} %all-to-all-done, s32[1024]{0:T(1024)S(1)} %pad_clamp_fusion.2), kind=kCustom, calls=%fused_computation.3 | custom fusion | bytes 6291712 | tf_op jit(solution)/shard_map/jit(_take)/gather | solution.py:83
  147.3 5.7 copy.48
  153.0 6.1 gather.31
  159.1 3.7 select_bitcast_fusion.1
  162.8 8.1 %copy.49 = f32[3,1,8,64,8,64]{5,4,3,2,0,1:T(8,128)} copy(f32[3,1,8,64,8,64]{5,3,4,2,0,1:T(8,128)S(1)} %select_bitcast_fusion.1) | data formatting | bytes 6291456 | tf_op jit(solution)/shard_map/transpose | solution.py:86
  170.9 6.4 reshape.542
  177.3 13.6 %fusion.6 = f32[3,1024]{1,0:T(4,128)S(1)} fusion(f32[512,1024]{1,0:T(8,128)} %bitcast.155, f32[3,512,512]{2,1,0:T(8,128)} %reshape.542, f32[1,512,1024]{2,1,0:T(8,128)} %param.15), kind=kOutput, calls=%fused_computation.16 | convolution fusion | flops 9666819072 | bytes 7352320 | tf_op jit(solution)/shard_map/dkmn,knp->dkmp/dot_general | solution.py:87
  191.0 11.9 %fusion.32 = f32[3,1,512,512]{3,2,0,1:T(8,128)} fusion(f32[1,512,1024]{2,1,0:T(8,128)S(1)} %copy-done.12, f32[3,1024]{1,0:T(4,128)S(1)} %bitcast.152, f32[512,1024]{1,0:T(8,128)S(1)} %bitcast.156), kind=kOutput, calls=%fused_computation.47 | convolution fusion | flops 9665249280 | bytes 7352320 | tf_op jit(solution)/shard_map/dkmp,knp->dkmn/dot_general | solution.py:91
  202.9 5.8 reshape.543
  208.7 6.6 copy.70
  215.3 5.9 reshape.544
  221.1 6.0 copy.51
  227.1 11.9 %gather_fusion.2 = f32[128,3,4096]{2,1,0:T(4,128)} fusion(f32[3,64,4096]{2,0,1:T(4,128)} %copy.51, s32[1024]{0:T(1024)S(1)} %pad_clamp_fusion.1), kind=kCustom, calls=%fused_computation.4 | custom fusion | bytes 12583424 | tf_op jit(solution)/shard_map/jit(_take)/gather | solution.py:107
  239.1 11.6 %select_bitcast_fusion = f32[3,128,4096]{2,0,1:T(4,128)} fusion(f32[128,3,4096]{2,1,0:T(4,128)} %gather_fusion.2, pred[128]{0:T(512)(128)(4,1)S(1)} %fusion.61, pred[128]{0:T(512)(128)(4,1)S(1)} %compare_and_fusion), kind=kLoop, calls=%fused_computation.14 | loop fusion | flops 3145728 | bytes 12583168 | tf_op jit(solution)/shard_map/jit(_where)/select_n | solution.py:106
  250.7 8.1 %all-to-all-start.1 = ((f32[3,128,4096]{2,0,1:T(4,128)}), f32[3,128,4096]{2,0,1:T(4,128)}, u32[]{:S(2)}, u32[]{:S(2)}) async-start(f32[3,128,4096]{2,0,1:T(4,128)} %select_bitcast_fusion), calls=%async_computation.1 | async-start | bytes 16777216 | tf_op jit(solution)/shard_map/all_to_all | solution.py:109
  258.9 2.3 dynamic-slice_select_fusion.1
  261.3 107.4 %all-to-all-done.1 = f32[3,128,4096]{2,0,1:T(4,128)} async-done(((f32[3,128,4096]{2,0,1:T(4,128)}), f32[3,128,4096]{2,0,1:T(4,128)}, u32[]{:S(2)}, u32[]{:S(2)}) %all-to-all-start.1) | async-done | bytes 6291488 | tf_op jit(solution)/shard_map/all_to_all | solution.py:109
  368.7 8.8 %fusion.15 = f32[3,32,4096]{2,1,0:T(8,128)S(1)} fusion(f32[3,128,4096]{2,0,1:T(4,128)} %all-to-all-done.1, s32[128]{0:T(128)S(1)} %fusion.77, s32[32]{0:T(128)S(1)} %copy-done.7), kind=kOutput, calls=%fused_computation.29 | convolution fusion | flops 603983872 | bytes 7864960 | tf_op jit(solution)/shard_map/ns,dnx->dsx/dot_general | solution.py:110
  377.6 2.4 reshape.545
  380.0 15.5 %convolution_bitcast_fusion.1 = f32[3,16,64,8,64]{4,1,2,0,3:T(8,128)} fusion(f32[3,32,64,64]{3,2,1,0:T(8,128)} %reshape.545, f32[32,16]{0,1:T(8,128)S(1)} %convert_bitcast_fusion, f32[32,8]{0,1:T(8,128)S(1)} %convert_bitcast_fusion.1), kind=kOutput, calls=%fused_computation.30 | convolution fusion | flops 603983872 | bytes 7867392 | tf_op jit(solution)/shard_map/rs,cs,dsab->dracb/dot_general | solution.py:119
  395.5 16.3 %copy.54 = f32[3,16,64,8,64]{4,3,2,1,0:T(8,128)} copy(f32[3,16,64,8,64]{4,1,2,0,3:T(8,128)} %convolution_bitcast_fusion.1) | data formatting | bytes 12582912 | tf_op jit(solution)/shard_map/rs,cs,dsab->dracb/transpose | solution.py:119
  411.8 11.5 %reshape.546 = f32[3,1024,512]{2,1,0:T(8,128)} reshape(f32[3,16,64,8,64]{4,3,2,1,0:T(8,128)} %copy.54) | data formatting | bytes 12582912 | tf_op jit(solution)/shard_map/reshape | solution.py:126
  423.3 13.5 %fusion.41 = f32[3,1024,512]{2,1,0:T(8,128)} fusion(f32[3,1024,512]{2,1,0:T(8,128)} %reshape.546, f32[512,512]{1,0:T(8,128)} %all-reduce.4.cloned.1.call-done), kind=kOutput, calls=%fused_computation.48 | convolution fusion | flops 9663676416 | bytes 13631488 | tf_op jit(solution)/shard_map/drc,co->dro/dot_general | solution.py:127
  436.9 0.4 all-reduce.8.cloned.1.call-start
  437.3 0.2 copy-done.8
  437.6 1.5 broadcast_subtract_fusion
  439.1 117.3 %all-reduce.6.cloned.1.call-done = f32[3,1024,512]{2,1,0:T(8,128)} async-done(((f32[3,1024,512]{2,1,0:T(8,128)}), f32[3,1024,512]{2,1,0:T(8,128)}) %all-reduce.6.cloned.1.call-update) | async-done | bytes 6291472 | tf_op jit(solution)/shard_map/psum | solution.py:128
  556.4 4.5 negate_divide_fusion
  560.9 2.6 copy-done.2
  563.5 2.0 dynamic-slice_select_fusion
  565.6 4.4 gather_fusion.5
  570.0 2.8 gather_fusion
  572.8 8.9 %gather_fusion.3 = f32[32,3,64,512]{3,2,1,0:T(8,128)} fusion(f32[3,16,64,512]{3,2,1,0:T(8,128)} %bitcast.146, s32[1024]{0:T(1024)S(1)} %pad_clamp_fusion), kind=kCustom, calls=%fused_computation.5 | custom fusion | bytes 25165952 | tf_op jit(solution)/shard_map/jit(_take)/gather | solution.py:134
  581.7 52.6 %all-reduce.8.cloned.1.call-done = f32[3,8,64,512]{3,2,1,0:T(8,128)} async-done(((f32[3,8,64,512]{3,2,1,0:T(8,128)}), f32[3,8,64,512]{3,2,1,0:T(8,128)}) %all-reduce.8.cloned.1.call-update) | async-done | bytes 3145744 | tf_op jit(solution)/shard_map/psum | solution.py:14
  634.3 7.7 %gather_fusion.4 = f32[32,3,64,512]{3,2,1,0:T(8,128)} fusion(f32[3,8,64,512]{3,2,1,0:T(8,128)} %all-reduce.8.cloned.1.call-done, s32[1024]{0:T(1024)S(1)} %pad_clamp_fusion.3), kind=kCustom, calls=%fused_computation.6 | custom fusion | bytes 25165952 | tf_op jit(solution)/shard_map/jit(_take)/gather | solution.py:136
  642.0 15.3 %fusion = f32[32,3,64,64]{3,2,1,0:T(8,128)S(1)} fusion(f32[32,3,64,512]{3,2,1,0:T(8,128)} %gather_fusion.4, pred[32]{0:T(512)(128)(4,1)S(1)} %get-tuple-element.10, f32[32,64,512]{2,1,0:T(8,128)} %gather_fusion.5, pred[32]{0:T(512)(128)(4,1)S(1)} %get-tuple-element.16), kind=kOutput, calls=%fused_computation.8 | convolution fusion | flops 2420113408 | bytes 18350144 | tf_op jit(solution)/shard_map/sao,dsbo->dsab/dot_general | solution.py:139
  657.4 15.4 %bitcast_add_fusion = f32[3,32,64,64]{2,3,0,1:T(8,128)} fusion(f32[32,3,64,64]{3,2,1,0:T(8,128)S(1)} %fusion, f32[32,3,64,512]{3,2,1,0:T(8,128)S(1)} %copy-done.3, pred[32]{0:T(512)(128)(4,1)S(1)} %get-tuple-element.16, f32[32,64,512]{2,1,0:T(8,128)S(1)} %copy-done.5, pred[32]{0:T(512)(128)(4,1)S(1)} %get-tuple-element.10), kind=kOutput, calls=%fused_computation.35 | convolution fusion | flops 2420506624 | bytes 19923008 | tf_op jit(solution)/shard_map/dsao,sbo->dsab/dot_general | solution.py:138
  672.7 3.6 copy.55
  676.3 3.3 reshape.550
  (61 shorter events, 0.9 us)
Async XLA Ops:
  6.5 5.6 copy-start
  23.1 116.1 %all-to-all-start = ((f32[3,128,4096]{2,0,1:T(4,128)}), f32[3,128,4096]{2,0,1:T(4,128)}, u32[]{:S(2)}, u32[]{:S(2)}) async-start(f32[3,128,4096]{2,0,1:T(4,128)} %copy.47), calls=%async_computation | async-start | bytes 16777216 | tf_op jit(solution)/shard_map/all_to_all | solution.py:71
  177.3 13.6 %copy-start.6 = (f32[3,1,1024]{2,1,0:T(1,128)S(1)}, f32[3,1,1024]{2,1,0:T(1,128)}, u32[]{:S(2)}) copy-start(f32[3,1,1024]{2,1,0:T(1,128)} %param.18) | copy-start | bytes 36868
  177.3 13.6 %copy-start.9 = (f32[1,1024]{1,0:T(1,128)S(1)}, f32[1,1024]{1,0:T(1,128)}, u32[]{:S(2)}) copy-start(f32[1,1024]{1,0:T(1,128)} %param.17) | copy-start | bytes 12292
  177.3 13.6 %copy-start.10 = (f32[1,1024]{1,0:T(1,128)S(1)}, f32[1,1024]{1,0:T(1,128)}, u32[]{:S(2)}) copy-start(f32[1,1024]{1,0:T(1,128)} %param.16) | copy-start | bytes 12292
  177.3 13.7 %copy-start.12 = (f32[1,512,1024]{2,1,0:T(8,128)S(1)}, f32[1,512,1024]{2,1,0:T(8,128)}, u32[]{:S(2)}) copy-start(f32[1,512,1024]{2,1,0:T(8,128)} %param.15) | copy-start | bytes 6291460
  250.7 10.6 %copy-start.7 = (s32[32]{0:T(128)S(1)}, s32[32]{0:T(128)}, u32[]{:S(2)}) copy-start(s32[32]{0:T(128)} %param.13) | copy-start | bytes 388
  250.7 118.0 %all-to-all-start.1 = ((f32[3,128,4096]{2,0,1:T(4,128)}), f32[3,128,4096]{2,0,1:T(4,128)}, u32[]{:S(2)}, u32[]{:S(2)}) async-start(f32[3,128,4096]{2,0,1:T(4,128)} %select_bitcast_fusion), calls=%async_computation.1 | async-start | bytes 16777216 | tf_op jit(solution)/shard_map/all_to_all | solution.py:109
  258.8 164.5 %all-reduce.4.cloned.1.call-start = ((), (), s32[]{:S(2)}) async-start(), calls=%async_computation.2 | async-start | bytes 2097152 | tf_op jit(solution)/shard_map/psum | solution.py:14
  261.2 295.2 %all-reduce.6.cloned.1.call-start = ((), (), s32[]{:S(2)}) async-start(), calls=%async_computation.3 | async-start | bytes 12582912 | tf_op jit(solution)/shard_map/psum | solution.py:128
  436.9 0.7 copy-start.8
  436.9 0.7 copy-start.11
  436.9 197.4 %all-reduce.8.cloned.1.call-start = ((), (), s32[]{:S(2)}) async-start(), calls=%async_computation.4 | async-start | bytes 6291456 | tf_op jit(solution)/shard_map/psum | solution.py:14
  560.9 2.6 copy-start.2
  565.6 4.5 copy-start.4
  642.0 15.3 %copy-start.3 = (f32[32,3,64,512]{3,2,1,0:T(8,128)S(1)}, f32[32,3,64,512]{3,2,1,0:T(8,128)}, u32[]{:S(2)}) copy-start(f32[32,3,64,512]{3,2,1,0:T(8,128)} %gather_fusion.3) | copy-start | bytes 37748740
  642.0 15.3 %copy-start.5 = (f32[32,64,512]{2,1,0:T(8,128)S(1)}, f32[32,64,512]{2,1,0:T(8,128)}, u32[]{:S(2)}) copy-start(f32[32,64,512]{2,1,0:T(8,128)} %gather_fusion) | copy-start | bytes 12582916
  657.3 22.2 %copy-start.1 = (f32[3,32,4096]{2,1,0:T(8,128)S(1)}, f32[3,32,4096]{2,1,0:T(8,128)}, u32[]{:S(2)}) copy-start(f32[3,32,4096]{2,1,0:T(8,128)} %param.12) | copy-start | bytes 4718596
Sparse Core Ops, SparseCore 0:
  262.0 87.8 all-reduce.3
  437.0 119.3 all-reduce.5
  565.7 68.6 all-reduce.7
where the time goes:
time: 694 us; the launch traced here: 686 us
  waiting for transfers between devices  381 us (55%)
  local copies, waits for them, and re-layouts  146 us (21%)
  matrix products  97.3 us (14%)
  other arithmetic  27.9 us (4%)
  starting transfers between devices  20.8 us (3%)
  between operations  13.6 us (2%)
    psum x1, waiting for transfers between devices, local(): summed_rows = lax.psum(partial_rows, 'col')  117 us
    all_to_all x1, waiting for transfers between devices, local(): lax.all_to_all(returning, ('row', 'col'), split_axis=1, concat_axis=1, ti...  107 us
    all_to_all x1, waiting for transfers between devices, local(): lax.all_to_all(outgoing, ('row', 'col'), split_axis=1, concat_axis=1, til...  103 us
    psum x2, waiting for transfers between devices, from_root(): return lax.psum(kept, axis)  52.6 us
    gather x3, local copies, waits for them, and re-layouts, local(): jnp.take(arrived, lookup.reshape(-1), axis=1)  19.9 us
    transpose x1, local copies, waits for them, and re-layouts, local(): jnp.einsum('rs,cs,dsab->dracb', row_hot, col_hot, ham_listed.reshape(3, t...  16.3 us
    dot_general x1, matrix products, local(): jnp.einsum('rs,cs,dsab->dracb', row_hot, col_hot, ham_listed.reshape(3, t...  15.5 us
    dot_general x1, matrix products, local(): renewed = jnp.einsum('dsao,sbo->dsab', x_rows, c_cols, precision=PRECISE)  15.4 us
  transfers between devices with their start and end apart: 5, of which 4 were waited for; matrix products, arithmetic and copies ran while one was open for 11% of the time, Pallas kernels for 0%

commit v1 on v0

--- a/solution.py
+++ b/solution.py
@@ -125,7 +125,11 @@
     )
     block_matrix = block_matrix.reshape(3, row_blocks * TILE, col_width)
     partial_rows = jnp.einsum("drc,co->dro", block_matrix, orbital_cols, precision=PRECISE)
-    summed_rows = lax.psum(partial_rows, "col")
+    summed_rows = partial_rows
+    for hop in (1, 2, 4, 8):
+        summed_rows = summed_rows + lax.ppermute(
+            summed_rows, "col", [(dev, dev ^ hop) for dev in range(16)]
+        )
     response_orbs = -summed_rows / (precond_diag[:, None] - orbital_energy[None, :])
     response_piece = lax.dynamic_slice_in_dim(
         response_orbs, own_col % col_ratio * col_width, col_width, 1

time: 694 us -> 1140 us (1.64)
  waiting for transfers between devices: 381 us -> 799 us
  other arithmetic: 27.9 us -> 41.8 us
    ppermute x0 -> x4, waiting for transfers between devices: none -> 535 us  [local(): lax.ppermute(summed_rows, 'col', [(dev, dev ^ hop) for dev in range(16)])]
    psum x1 -> x0, waiting for transfers between devices: 117 us -> none  [local(): summed_rows = lax.psum(partial_rows, 'col')]
    add x0 -> x3, other arithmetic: none -> 13 us  [local(): summed_rows + lax.ppermute(summed_rows, 'col', [(dev, dev ^ hop) for dev...]
    ppermute x0 -> x4, starting transfers between devices: none -> 11.8 us  [local(): lax.ppermute(summed_rows, 'col', [(dev, dev ^ hop) for dev in range(16)])]
  transfers between devices with their start and end apart: 5 -> 8, of which waited for: 4 -> 7; matrix products, arithmetic and copies ran while one was open for 11% -> 7% of each run, Pallas kernels for 0% -> 0%
where the time goes in v1:
time: 1140 us; the launch traced here: 1130 us
  waiting for transfers between devices  799 us (70%)
  local copies, waits for them, and re-layouts  145 us (13%)
  matrix products  97.4 us (9%)
  other arithmetic  41.8 us (4%)
  starting transfers between devices  31.9 us (3%)
  between operations  14 us (1%)
    ppermute x4, waiting for transfers between devices, local(): lax.ppermute(summed_rows, 'col', [(dev, dev ^ hop) for dev in range(16)])  535 us
    all_to_all x1, waiting for transfers between devices, local(): lax.all_to_all(returning, ('row', 'col'), split_axis=1, concat_axis=1, ti...  107 us
    all_to_all x1, waiting for transfers between devices, local(): lax.all_to_all(outgoing, ('row', 'col'), split_axis=1, concat_axis=1, til...  103 us
    psum x2, waiting for transfers between devices, from_root(): return lax.psum(kept, axis)  52.2 us
  transfers between devices with their start and end apart: 8, of which 7 were waited for; matrix products, arithmetic and copies ran while one was open for 7% of the time, Pallas kernels for 0%

profile of v1, /device:TPU:0, one launch (start us, length us, event | category | flops | bytes accessed | tf_op | source)
XLA Modules:
  0.0 1129.2 jit_solution(2764481185531145050)
XLA Ops:
  12.1 3.4 convolution_bitcast_fusion
  15.5 7.5 copy.47
  23.1 11.9 %all-to-all-start = ((f32[3,128,4096]{2,0,1:T(4,128)}), f32[3,128,4096]{2,0,1:T(4,128)}, u32[]{:S(2)}, u32[]{:S(2)}) async-start(f32[3,128,4096]{2,0,1:T(4,128)} %copy.47), calls=%async_computation | async-start | bytes 16777216 | tf_op jit(solution)/shard_map/all_to_all | solution.py:71
  35.4 103.5 %all-to-all-done = f32[3,128,4096]{2,0,1:T(4,128)} async-done(((f32[3,128,4096]{2,0,1:T(4,128)}), f32[3,128,4096]{2,0,1:T(4,128)}, u32[]{:S(2)}, u32[]{:S(2)}) %all-to-all-start) | async-done | bytes 6291488 | tf_op jit(solution)/shard_map/all_to_all | solution.py:71
  138.9 8.1 gather_fusion.1
  147.0 5.7 copy.48
  152.7 6.1 gather.31
  158.8 3.7 select_bitcast_fusion.1
  162.5 8.1 copy.49
  170.6 6.5 reshape.542
  177.1 13.6 %fusion.6 = f32[3,1024]{1,0:T(4,128)S(1)} fusion(f32[512,1024]{1,0:T(8,128)} %bitcast.155, f32[3,512,512]{2,1,0:T(8,128)} %reshape.542, f32[1,512,1024]{2,1,0:T(8,128)} %param.15), kind=kOutput, calls=%fused_computation.16 | convolution fusion | flops 9666819072 | bytes 7352320 | tf_op jit(solution)/shard_map/dkmn,knp->dkmp/dot_general | solution.py:87
  190.7 11.9 %fusion.32 = f32[3,1,512,512]{3,2,0,1:T(8,128)} fusion(f32[1,512,1024]{2,1,0:T(8,128)S(1)} %copy-done.13, f32[3,1024]{1,0:T(4,128)S(1)} %bitcast.152, f32[512,1024]{1,0:T(8,128)S(1)} %bitcast.156), kind=kOutput, calls=%fused_computation.47 | convolution fusion | flops 9665249280 | bytes 7352320 | tf_op jit(solution)/shard_map/dkmp,knp->dkmn/dot_general | solution.py:91
  202.6 6.0 reshape.543
  208.6 6.6 copy.70
  215.2 5.9 reshape.544
  221.0 6.0 copy.51
  227.0 11.7 %gather_fusion.2 = f32[128,3,4096]{2,1,0:T(4,128)} fusion(f32[3,64,4096]{2,0,1:T(4,128)} %copy.51, s32[1024]{0:T(1024)S(1)} %pad_clamp_fusion.1), kind=kCustom, calls=%fused_computation.4 | custom fusion | bytes 12583424 | tf_op jit(solution)/shard_map/jit(_take)/gather | solution.py:107
  238.7 11.6 %select_bitcast_fusion = f32[3,128,4096]{2,0,1:T(4,128)} fusion(f32[128,3,4096]{2,1,0:T(4,128)} %gather_fusion.2, pred[128]{0:T(512)(128)(4,1)S(1)} %fusion.61, pred[128]{0:T(512)(128)(4,1)S(1)} %compare_and_fusion), kind=kLoop, calls=%fused_computation.14 | loop fusion | flops 3145728 | bytes 12583168 | tf_op jit(solution)/shard_map/jit(_where)/select_n | solution.py:106
  250.4 8.1 all-to-all-start.1
  258.6 2.3 dynamic-slice_select_fusion.1
  261.0 107.4 %all-to-all-done.1 = f32[3,128,4096]{2,0,1:T(4,128)} async-done(((f32[3,128,4096]{2,0,1:T(4,128)}), f32[3,128,4096]{2,0,1:T(4,128)}, u32[]{:S(2)}, u32[]{:S(2)}) %all-to-all-start.1) | async-done | bytes 6291488 | tf_op jit(solution)/shard_map/all_to_all | solution.py:109
  368.4 8.8 fusion.15
  377.3 2.4 reshape.545
  379.7 15.5 %convolution_bitcast_fusion.1 = f32[3,16,64,8,64]{4,1,2,0,3:T(8,128)} fusion(f32[3,32,64,64]{3,2,1,0:T(8,128)} %reshape.545, f32[32,16]{0,1:T(8,128)S(1)} %convert_bitcast_fusion, f32[32,8]{0,1:T(8,128)S(1)} %convert_bitcast_fusion.1), kind=kOutput, calls=%fused_computation.30 | convolution fusion | flops 603983872 | bytes 7867392 | tf_op jit(solution)/shard_map/rs,cs,dsab->dracb/dot_general | solution.py:119
  395.2 16.3 %copy.54 = f32[3,16,64,8,64]{4,3,2,1,0:T(8,128)} copy(f32[3,16,64,8,64]{4,1,2,0,3:T(8,128)} %convolution_bitcast_fusion.1) | data formatting | bytes 12582912 | tf_op jit(solution)/shard_map/rs,cs,dsab->dracb/transpose | solution.py:119
  411.5 11.5 %reshape.546 = f32[3,1024,512]{2,1,0:T(8,128)} reshape(f32[3,16,64,8,64]{4,3,2,1,0:T(8,128)} %copy.54) | data formatting | bytes 12582912 | tf_op jit(solution)/shard_map/reshape | solution.py:126
  423.0 13.6 %fusion.41 = f32[3,1024,512]{2,1,0:T(8,128)S(1)} fusion(f32[3,1024,512]{2,1,0:T(8,128)} %reshape.546, f32[512,512]{1,0:T(8,128)} %all-reduce.3.cloned.1.call-done), kind=kOutput, calls=%fused_computation.48 | convolution fusion | flops 9663676416 | bytes 13631488 | tf_op jit(solution)/shard_map/drc,co->dro/dot_general | solution.py:127
  437.1 133.3 %collective-permute-done = f32[3,1024,512]{2,1,0:T(8,128)} collective-permute-done((f32[3,1024,512]{2,1,0:T(8,128)S(1)}, f32[3,1024,512]{2,1,0:T(8,128)}, u32[]{:S(2)}, u32[]{:S(2)}) %collective-permute-start) | collective-permute-done | bytes 6291488 | tf_op jit(solution)/shard_map/ppermute | solution.py:130
  570.4 4.3 add.247
  576.1 133.1 %collective-permute-done.1 = f32[3,1024,512]{2,1,0:T(8,128)} collective-permute-done((f32[3,1024,512]{2,1,0:T(8,128)S(1)}, f32[3,1024,512]{2,1,0:T(8,128)}, u32[]{:S(2)}, u32[]{:S(2)}) %collective-permute-start.1) | collective-permute-done | bytes 6291488 | tf_op jit(solution)/shard_map/ppermute | solution.py:130
  709.2 4.3 add.248
  713.5 4.3 collective-permute-start.2
  717.8 134.9 %collective-permute-done.2 = f32[3,1024,512]{2,1,0:T(8,128)} collective-permute-done((f32[3,1024,512]{2,1,0:T(8,128)S(1)}, f32[3,1024,512]{2,1,0:T(8,128)}, u32[]{:S(2)}, u32[]{:S(2)}) %collective-permute-start.2) | collective-permute-done | bytes 6291488 | tf_op jit(solution)/shard_map/ppermute | solution.py:130
  852.7 4.3 add.249
  857.1 5.7 collective-permute-start.3
  863.0 134.2 %collective-permute-done.3 = f32[3,1024,512]{2,1,0:T(8,128)} collective-permute-done((f32[3,1024,512]{2,1,0:T(8,128)S(1)}, f32[3,1024,512]{2,1,0:T(8,128)}, u32[]{:S(2)}, u32[]{:S(2)}) %collective-permute-start.3) | collective-permute-done | bytes 6291488 | tf_op jit(solution)/shard_map/ppermute | solution.py:130
  997.2 6.6 negate_divide_fusion
  1003.9 2.6 copy-done.2
  1006.4 2.1 dynamic-slice_select_fusion
  1008.7 4.4 gather_fusion.5
  1013.1 2.8 gather_fusion
  1015.9 8.7 gather_fusion.3
  1024.6 52.2 %all-reduce.5.cloned.1.call-done = f32[3,8,64,512]{3,2,1,0:T(8,128)} async-done(((f32[3,8,64,512]{3,2,1,0:T(8,128)}), f32[3,8,64,512]{3,2,1,0:T(8,128)}) %all-reduce.5.cloned.1.call-update) | async-done | bytes 3145744 | tf_op jit(solution)/shard_map/psum | solution.py:14
  1076.8 7.7 gather_fusion.4
  1084.5 15.3 %fusion = f32[32,3,64,64]{3,2,1,0:T(8,128)S(1)} fusion(f32[32,3,64,512]{3,2,1,0:T(8,128)} %gather_fusion.4, pred[32]{0:T(512)(128)(4,1)S(1)} %get-tuple-element.10, f32[32,64,512]{2,1,0:T(8,128)} %gather_fusion.5, pred[32]{0:T(512)(128)(4,1)S(1)} %get-tuple-element.16), kind=kOutput, calls=%fused_computation.8 | convolution fusion | flops 2420113408 | bytes 18350144 | tf_op jit(solution)/shard_map/sao,dsbo->dsab/dot_general | solution.py:143
  1099.9 15.4 %bitcast_add_fusion = f32[3,32,64,64]{2,3,0,1:T(8,128)} fusion(f32[32,3,64,64]{3,2,1,0:T(8,128)S(1)} %fusion, f32[32,3,64,512]{3,2,1,0:T(8,128)S(1)} %copy-done.3, pred[32]{0:T(512)(128)(4,1)S(1)} %get-tuple-element.16, f32[32,64,512]{2,1,0:T(8,128)S(1)} %copy-done.6, pred[32]{0:T(512)(128)(4,1)S(1)} %get-tuple-element.10), kind=kOutput, calls=%fused_computation.35 | convolution fusion | flops 2420506624 | bytes 19923008 | tf_op jit(solution)/shard_map/dsao,sbo->dsab/dot_general | solution.py:142
  1115.2 3.6 copy.55
  1118.8 3.3 reshape.550
  (71 shorter events, 8.4 us)
Async XLA Ops:
  6.5 5.6 copy-start
  23.1 115.8 %all-to-all-start = ((f32[3,128,4096]{2,0,1:T(4,128)}), f32[3,128,4096]{2,0,1:T(4,128)}, u32[]{:S(2)}, u32[]{:S(2)}) async-start(f32[3,128,4096]{2,0,1:T(4,128)} %copy.47), calls=%async_computation | async-start | bytes 16777216 | tf_op jit(solution)/shard_map/all_to_all | solution.py:71
  177.1 13.6 %copy-start.7 = (f32[3,1,1024]{2,1,0:T(1,128)S(1)}, f32[3,1,1024]{2,1,0:T(1,128)}, u32[]{:S(2)}) copy-start(f32[3,1,1024]{2,1,0:T(1,128)} %param.18) | copy-start | bytes 36868
  177.1 13.6 %copy-start.10 = (f32[1,1024]{1,0:T(1,128)S(1)}, f32[1,1024]{1,0:T(1,128)}, u32[]{:S(2)}) copy-start(f32[1,1024]{1,0:T(1,128)} %param.17) | copy-start | bytes 12292
  177.1 13.6 %copy-start.11 = (f32[1,1024]{1,0:T(1,128)S(1)}, f32[1,1024]{1,0:T(1,128)}, u32[]{:S(2)}) copy-start(f32[1,1024]{1,0:T(1,128)} %param.16) | copy-start | bytes 12292
  177.1 13.6 %copy-start.13 = (f32[1,512,1024]{2,1,0:T(8,128)S(1)}, f32[1,512,1024]{2,1,0:T(8,128)}, u32[]{:S(2)}) copy-start(f32[1,512,1024]{2,1,0:T(8,128)} %param.15) | copy-start | bytes 6291460
  250.4 10.6 copy-start.8
  250.4 118.0 %all-to-all-start.1 = ((f32[3,128,4096]{2,0,1:T(4,128)}), f32[3,128,4096]{2,0,1:T(4,128)}, u32[]{:S(2)}, u32[]{:S(2)}) async-start(f32[3,128,4096]{2,0,1:T(4,128)} %select_bitcast_fusion), calls=%async_computation.1 | async-start | bytes 16777216 | tf_op jit(solution)/shard_map/all_to_all | solution.py:109
  258.5 164.6 %all-reduce.3.cloned.1.call-start = ((), (), s32[]{:S(2)}) async-start(), calls=%async_computation.2 | async-start | bytes 2097152 | tf_op jit(solution)/shard_map/psum | solution.py:14
  260.9 815.9 %all-reduce.5.cloned.1.call-start = ((), (), s32[]{:S(2)}) async-start(), calls=%async_computation.3 | async-start | bytes 6291456 | tf_op jit(solution)/shard_map/psum | solution.py:14
  436.6 133.8 %collective-permute-start = (f32[3,1024,512]{2,1,0:T(8,128)S(1)}, f32[3,1024,512]{2,1,0:T(8,128)}, u32[]{:S(2)}, u32[]{:S(2)}) collective-permute-start(f32[3,1024,512]{2,1,0:T(8,128)S(1)} %fusion.41), channel_id=1, source_target_pairs={{0,1},{1,0},{2,3},{3,2},{4,5},{5,4},{6,7},{7,6},{8,9},{9,8},{10,11... | collective-permute-start | bytes 18874376 | tf_op jit(solution)/shard_map/ppermute | solution.py:130
  574.7 134.4 %collective-permute-start.1 = (f32[3,1024,512]{2,1,0:T(8,128)S(1)}, f32[3,1024,512]{2,1,0:T(8,128)}, u32[]{:S(2)}, u32[]{:S(2)}) collective-permute-start(f32[3,1024,512]{2,1,0:T(8,128)S(1)} %add.247), channel_id=1, source_target_pairs={{0,2},{1,3},{2,0},{3,1},{4,6},{5,7},{6,4},{7,5},{8,10},{9,11},{10,... | collective-permute-start | bytes 18874376 | tf_op jit(solution)/shard_map/ppermute | solution.py:130
  713.5 149.2 %copy-start.9 = (f32[1024]{0:T(1024)S(1)}, f32[1024]{0:T(1024)}, u32[]{:S(2)}) copy-start(f32[1024]{0:T(1024)} %param.20) | copy-start | bytes 12292
  713.5 149.2 %copy-start.12 = (f32[512]{0:T(512)S(1)}, f32[512]{0:T(512)}, u32[]{:S(2)}) copy-start(f32[512]{0:T(512)} %param.21) | copy-start | bytes 6148
  713.5 139.2 %collective-permute-start.2 = (f32[3,1024,512]{2,1,0:T(8,128)S(1)}, f32[3,1024,512]{2,1,0:T(8,128)}, u32[]{:S(2)}, u32[]{:S(2)}) collective-permute-start(f32[3,1024,512]{2,1,0:T(8,128)S(1)} %add.248), channel_id=1, source_target_pairs={{0,4},{1,5},{2,6},{3,7},{4,0},{5,1},{6,2},{7,3},{8,12},{9,13},{10,... | collective-permute-start | bytes 18874376 | tf_op jit(solution)/shard_map/ppermute | solution.py:130
  857.1 5.9 copy-start.5
  857.1 140.1 %collective-permute-start.3 = (f32[3,1024,512]{2,1,0:T(8,128)S(1)}, f32[3,1024,512]{2,1,0:T(8,128)}, u32[]{:S(2)}, u32[]{:S(2)}) collective-permute-start(f32[3,1024,512]{2,1,0:T(8,128)S(1)} %add.249), channel_id=1, source_target_pairs={{0,8},{1,9},{2,10},{3,11},{4,12},{5,13},{6,14},{7,15},{8,0},{9,1},... | collective-permute-start | bytes 18874376 | tf_op jit(solution)/shard_map/ppermute | solution.py:130
  1003.8 2.6 copy-start.2
  1008.6 4.4 copy-start.4
  1084.5 15.3 %copy-start.3 = (f32[32,3,64,512]{3,2,1,0:T(8,128)S(1)}, f32[32,3,64,512]{3,2,1,0:T(8,128)}, u32[]{:S(2)}) copy-start(f32[32,3,64,512]{3,2,1,0:T(8,128)} %gather_fusion.3) | copy-start | bytes 37748740
  1084.5 15.3 %copy-start.6 = (f32[32,64,512]{2,1,0:T(8,128)S(1)}, f32[32,64,512]{2,1,0:T(8,128)}, u32[]{:S(2)}) copy-start(f32[32,64,512]{2,1,0:T(8,128)} %gather_fusion) | copy-start | bytes 12582916
  1099.8 22.2 %copy-start.1 = (f32[3,32,4096]{2,1,0:T(8,128)S(1)}, f32[3,32,4096]{2,1,0:T(8,128)}, u32[]{:S(2)}) copy-start(f32[3,32,4096]{2,1,0:T(8,128)} %param.12) | copy-start | bytes 4718596
Sparse Core Ops, SparseCore 0:
  261.6 87.8 all-reduce.2
  1008.7 67.9 all-reduce.4
